TPU v7x, 512 devices: a whole 4x8x8 slice. The times are simulated.
512 devices in a mesh: dp: 32 (over z_hi, y, core), seq: 16 (over z_lo, x).
Axes of the slice: x: 4, y: 8, z: 8 (z_hi: 2, z_lo: 4; z = z_hi * 4 + z_lo), core: 2. Of those that a mesh axis runs over, the one named last changes fastest.
Arguments:
- img_qkv: bfloat16 [32, 1792, 3, 2048], P('dp', 'seq'), may hold values from -6 to 6
- txt_qkv: bfloat16 [32, 256, 3, 2048], P('dp', 'seq'), may hold values from -6 to 6
- img_cot: bfloat16 [32, 1792, 2048], P('dp', 'seq'), may hold values from -48 to 48
- txt_cot: bfloat16 [32, 256, 2048], P('dp', 'seq'), may hold values from -48 to 48
- norm_gains: float32 [4, 128], replicated, may hold values from 0.5 to 2
Outputs:
- img_out: bfloat16 [32, 1792, 2048], P('dp', 'seq')
- txt_out: bfloat16 [32, 256, 2048], P('dp', 'seq')
- img_grad: bfloat16 [32, 1792, 3, 2048], P('dp', 'seq')
- txt_grad: bfloat16 [32, 256, 3, 2048], P('dp', 'seq')
- gain_grad: float32 [512], P('dp')
All inputs are finite; a program needn't handle non-finite values.
Results may differ from a plain program's by a relative error of at most 0.012.
The roundings to bfloat16 on the way count: a program that leaves them out, or rounds other values in their place, can miss the bound.
Values may be sent and summed in bfloat16 or wider, within the bound.
A program may use at most 128 MiB of HBM per device.

v0:
```python
import math
import jax
import jax.numpy as jnp
from jax import lax
from jax.sharding import PartitionSpec as P

HD = 128
GRID_W = 64
EPSILON = 1e-06


def rope_tables(seq_len, text_len, grid_w, head_dim):
    position = jnp.arange(seq_len, dtype=jnp.int32)
    image_pos = jnp.maximum(position - text_len, 0)
    image_col = (position >= text_len).astype(jnp.float32)
    row_pos = (image_pos // grid_w).astype(jnp.float32) * image_col
    col_pos = (image_pos % grid_w).astype(jnp.float32) * image_col
    time_dims = head_dim // 8
    axis_dims = (head_dim - time_dims) // 2
    channel = jnp.arange(head_dim, dtype=jnp.int32)
    in_rows = (channel >= time_dims) & (channel < time_dims + axis_dims)
    in_cols = channel >= time_dims + axis_dims
    within = jnp.where(in_cols, channel - time_dims - axis_dims, channel - time_dims)
    within = jnp.maximum(within, 0) // 2
    frequency = jnp.power(jnp.float32(10000.0), -2.0 * within.astype(jnp.float32) / axis_dims)
    angles = jnp.where(in_rows[None, :], row_pos[:, None] * frequency[None, :], jnp.float32(0.0))
    angles = jnp.where(in_cols[None, :], col_pos[:, None] * frequency[None, :], angles)
    even_lane = (channel % 2 == 0)[None, :]
    return (jnp.cos(angles), jnp.sin(angles), even_lane, image_col[:, None])


def rms_rows(values_in):
    inverse = lax.rsqrt(jnp.mean(values_in * values_in, axis=-1, keepdims=True) + EPSILON)
    return (values_in * inverse, inverse)


def rms_back(grad_hat, hat_vals, inverse):
    middle = jnp.mean(grad_hat * hat_vals, axis=-1, keepdims=True)
    return (grad_hat - hat_vals * middle) * inverse


def rotate(values_in, tables):
    cos_t, sin_t, even_lane, image_col = tables
    following = jnp.roll(values_in, -1, axis=-1)
    preceding = jnp.roll(values_in, 1, axis=-1)
    turned = jnp.where(even_lane, -following, preceding)
    return values_in * cos_t + turned * sin_t


def unrotate(grad_in, tables):
    cos_t, sin_t, even_lane, image_col = tables
    scaled = grad_in * sin_t
    following = jnp.roll(scaled, -1, axis=-1)
    preceding = jnp.roll(scaled, 1, axis=-1)
    turned = jnp.where(even_lane, following, -preceding)
    return grad_in * cos_t + turned


def head_pass(q_raw, k_raw, value, d_out, norm_gains, tables, n_blocks):
    image_col = tables[3]
    seq_len, head_dim = q_raw.shape
    attn_scale = 1.0 / math.sqrt(head_dim)
    q_hat, q_inv = rms_rows(q_raw)
    k_hat, k_inv = rms_rows(k_raw)
    q_gain = jnp.where(image_col > 0.5, norm_gains[0][None, :], norm_gains[2][None, :])
    k_gain = jnp.where(image_col > 0.5, norm_gains[1][None, :], norm_gains[3][None, :])
    q_rot = rotate(q_hat * q_gain, tables).astype(jnp.bfloat16)
    k_rot = rotate(k_hat * k_gain, tables).astype(jnp.bfloat16)
    block_rows = seq_len // n_blocks
    contract_last = (((1,), (1,)), ((), ()))
    contract_first = (((0,), (0,)), ((), ()))

    def block_step(pieces):
        q_block, d_block = pieces
        scores = (
            lax.dot_general(q_block, k_rot, contract_last, preferred_element_type=jnp.float32)
            * attn_scale
        )
        exp_scores = jnp.exp(scores)
        row_sum = jnp.sum(exp_scores, axis=1, keepdims=True)
        prob_half = (exp_scores / row_sum).astype(jnp.bfloat16)
        out_block = jnp.dot(prob_half, value, preferred_element_type=jnp.float32).astype(
            jnp.bfloat16
        )
        row_delta = jnp.sum(
            d_block.astype(jnp.float32) * out_block.astype(jnp.float32), axis=1, keepdims=True
        )
        d_prob = lax.dot_general(d_block, value, contract_last, preferred_element_type=jnp.float32)
        d_score = (exp_scores / row_sum * (d_prob - row_delta) * attn_scale).astype(jnp.bfloat16)
        return (out_block, prob_half, d_score)

    q_blocks = q_rot.reshape(n_blocks, block_rows, head_dim)
    d_blocks = d_out.reshape(n_blocks, block_rows, head_dim)
    out_blocks, prob_blocks, score_blocks = lax.map(block_step, (q_blocks, d_blocks))
    attn_out = out_blocks.reshape(seq_len, head_dim)
    prob_all = prob_blocks.reshape(seq_len, seq_len)
    d_score_all = score_blocks.reshape(seq_len, seq_len)
    d_value = lax.dot_general(prob_all, d_out, contract_first, preferred_element_type=jnp.float32)
    dq_rot = jnp.dot(d_score_all, k_rot, preferred_element_type=jnp.float32)
    dk_rot = lax.dot_general(d_score_all, q_rot, contract_first, preferred_element_type=jnp.float32)
    dq_norm = unrotate(dq_rot, tables)
    dk_norm = unrotate(dk_rot, tables)
    text_col = 1.0 - image_col
    gain_terms = jnp.stack(
        [
            jnp.sum(dq_norm * q_hat * image_col, axis=0),
            jnp.sum(dk_norm * k_hat * image_col, axis=0),
            jnp.sum(dq_norm * q_hat * text_col, axis=0),
            jnp.sum(dk_norm * k_hat * text_col, axis=0),
        ]
    )
    d_query = rms_back(dq_norm * q_gain, q_hat, q_inv).astype(jnp.bfloat16)
    d_key = rms_back(dk_norm * k_gain, k_hat, k_inv).astype(jnp.bfloat16)
    packed = jnp.stack([d_query, d_key, d_value.astype(jnp.bfloat16), attn_out], axis=1)
    return (packed, gain_terms)


def per_device(img_qkv, txt_qkv, img_cot, txt_cot, norm_gains):
    seq_devices = lax.axis_size("seq")
    data_devices = lax.axis_size("dp")
    img_proj, txt_proj = (
        lax.all_to_all(img_qkv, "seq", split_axis=3, concat_axis=1, tiled=True),
        lax.all_to_all(txt_qkv, "seq", split_axis=3, concat_axis=1, tiled=True),
    )
    img_grad_in, txt_grad_in = (
        lax.all_to_all(img_cot, "seq", split_axis=2, concat_axis=1, tiled=True),
        lax.all_to_all(txt_cot, "seq", split_axis=2, concat_axis=1, tiled=True),
    )
    text_len = txt_proj.shape[1]
    joint = jnp.concatenate([txt_proj[0], img_proj[0]], axis=0)
    joint_cot = jnp.concatenate([txt_grad_in[0], img_grad_in[0]], axis=0)
    seq_len = joint.shape[0]
    head_dim = HD
    local_heads = joint.shape[2] // head_dim
    tables = rope_tables(seq_len, text_len, GRID_W, head_dim)
    n_blocks = max(1, seq_len // 512)
    packed, gain_terms = head_pass(
        joint[:, 0, 0:head_dim].astype(jnp.float32),
        joint[:, 1, 0:head_dim].astype(jnp.float32),
        joint[:, 2, 0:head_dim],
        joint_cot,
        norm_gains,
        tables,
        n_blocks,
    )
    txt_back = packed[None, :text_len]
    img_back = packed[None, text_len:]
    img_tokens, txt_tokens = (
        lax.all_to_all(img_back, "seq", split_axis=1, concat_axis=3, tiled=True),
        lax.all_to_all(txt_back, "seq", split_axis=1, concat_axis=3, tiled=True),
    )
    img_out = img_tokens[:, :, 3, :]
    txt_out = txt_tokens[:, :, 3, :]
    img_grad = img_tokens[:, :, 0:3, :]
    txt_grad = txt_tokens[:, :, 0:3, :]
    grad_scale = 1.0 / math.sqrt(data_devices * seq_len * local_heads * seq_devices)
    partial_grad = (gain_terms * grad_scale).reshape(4 * head_dim)
    summed = lax.psum(partial_grad, "seq")
    gain_grad = lax.psum_scatter(summed, "dp", scatter_dimension=0, tiled=True)
    return (img_out, txt_out, img_grad, txt_grad, gain_grad)


def solution(mesh):
    in_specs = (
        P("dp", "seq", None, None),
        P("dp", "seq", None, None),
        P("dp", "seq", None),
        P("dp", "seq", None),
        P(),
    )
    out_specs = (
        P("dp", "seq", None),
        P("dp", "seq", None),
        P("dp", "seq", None, None),
        P("dp", "seq", None, None),
        P("dp"),
    )
    return jax.shard_map(
        per_device, mesh=mesh, in_specs=in_specs, out_specs=out_specs, check_vma=False
    )
```

profile of v0, /device:TPU:2, one launch (start us, length us, event | category | flops | bytes accessed | tf_op | source)
XLA Modules:
  0.0 398.8 jit_solution(10600250610665582752)
XLA Ops:
  3.1 11.5 %reduce.9 = bf16[2048,16]{1,0:T(8,128)(2,1)S(1)} reduce(bf16[2048,1,16]{2,1,0:T(2,128)(2,1)S(1)} %bitcast.205, bf16[]{:T(256)} %broadcast.812), dimensions={1}, to_apply=%bitcast.165.reduce_sub_computation | reduce | bytes 131074
  15.9 10.3 %all-to-all-start.2 = ((bf16[16,2,1024]{2,1,0:T(2,128)(2,1)}), bf16[16,2,1024]{2,1,0:T(2,128)(2,1)S(1)}, u32[]{:S(2)}, u32[]{:S(2)}) async-start(bf16[16,2,1024]{2,1,0:T(2,128)(2,1)} %reshape.852), calls=%async_computation.2 | async-start | bytes 131072 | tf_op jit(solution)/shard_map/all_to_all | solution.py:127
  33.2 6.0 %all-to-all-start = ((bf16[16,2,3072]{2,1,0:T(2,128)(2,1)}), bf16[16,2,3072]{2,1,0:T(2,128)(2,1)S(1)}, u32[]{:S(2)}, u32[]{:S(2)}) async-start(bf16[16,2,3072]{2,1,0:T(2,128)(2,1)} %reshape.848), calls=%async_computation | async-start | bytes 393216 | tf_op jit(solution)/shard_map/all_to_all | solution.py:123
  41.6 11.5 %reduce.8 = bf16[2048,112]{1,0:T(8,128)(2,1)S(1)} reduce(bf16[2048,1,112]{2,1,0:T(2,128)(2,1)S(1)} %bitcast.206, bf16[]{:T(256)} %broadcast.812), dimensions={1}, to_apply=%bitcast.163.reduce_sub_computation | reduce | bytes 917506
  55.0 7.7 %all-to-all-start.3 = ((bf16[16,2,7168]{2,1,0:T(2,128)(2,1)}), bf16[16,2,7168]{2,1,0:T(2,128)(2,1)S(1)}, u32[]{:S(2)}, u32[]{:S(2)}) async-start(bf16[16,2,7168]{2,1,0:T(2,128)(2,1)} %reshape.850), calls=%async_computation.3 | async-start | bytes 917504 | tf_op jit(solution)/shard_map/all_to_all | solution.py:126
  65.2 9.2 %all-to-all-done.3 = bf16[16,2,7168]{2,1,0:T(2,128)(2,1)S(1)} async-done(((bf16[16,2,7168]{2,1,0:T(2,128)(2,1)}), bf16[16,2,7168]{2,1,0:T(2,128)(2,1)S(1)}, u32[]{:S(2)}, u32[]{:S(2)}) %all-to-all-start.3) | async-done | bytes 458784 | tf_op jit(solution)/shard_map/all_to_all | solution.py:126
  75.1 6.0 %all-to-all-start.1 = ((bf16[1,112,3,2048]{1,2,0,3:T(4,128)(2,1)}), bf16[1,112,3,2048]{1,2,0,3:T(4,128)(2,1)S(1)}, u32[]{:S(2)}, u32[]{:S(2)}) async-start(bf16[1,112,3,2048]{1,2,0,3:T(4,128)(2,1)} %copy.60), calls=%async_computation.1 | async-start | bytes 4194304 | tf_op jit(solution)/shard_map/all_to_all | solution.py:122
  85.2 4.2 %reshape.849 = bf16[2048,1,3,16]{3,2,1,0:T(4,128)(2,1)} reshape(bf16[16,2,3072]{2,1,0:T(2,128)(2,1)} %copy-done.15) | data formatting | bytes 393216
  99.3 21.8 %all-to-all-done.1 = bf16[1,112,3,2048]{1,2,0,3:T(4,128)(2,1)S(1)} async-done(((bf16[1,112,3,2048]{1,2,0,3:T(4,128)(2,1)}), bf16[1,112,3,2048]{1,2,0,3:T(4,128)(2,1)S(1)}, u32[]{:S(2)}, u32[]{:S(2)}) %all-to-all-start.1) | async-done | bytes 1376288 | tf_op jit(solution)/shard_map/all_to_all | solution.py:122
  128.0 5.9 %fusion.33 = (bf16[2048,128]{0,1:T(8,128)(2,1)}, f32[2048,128]{0,1:T(8,128)S(1)}) fusion(f32[2048,1]{0,1:T(1,128)S(1)} %get-tuple-element.142, f32[2048,127]{0,1:T(8,128)S(1)} %get-tuple-element.145, f32[2048,127]{0,1:T(8,128)S(1)} %get-tuple-element.144, f32[2048,1]{0,1:T(1,128)S(1)} %get-tuple-element.141, f32[2048]{0:T(1024)S(1)} %get-tuple-element.161, ...), kind=kLoop, calls=%fused_computation.55 | loop fusion | flops 5242880 | bytes 4756352 | tf_op jit(solution)/shard_map/convert_element_type | solution.py:68
  150.0 7.8 %fusion.29 = bf16[4,512,128]{2,1,0:T(8,128)(2,1)S(1)} fusion(f32[4,512,1]{2,1,0:T(8,128)} %concatenate.120, f32[4,512,127]{2,1,0:T(8,128)} %bitcast.210, f32[4,512,127]{2,1,0:T(8,128)} %bitcast.211, f32[4,512,1]{2,1,0:T(8,128)} %concatenate.121, f32[4,512,128]{2,1,0:T(8,128)S(1)} %bitcast.209, f32[4,512]{1,0:T(4,128)S(1)} %copy-done.28, ...), kind=kLoop, calls=%fused_computation.50 | loop fusion | flops 3932160 | bytes 3698560 | tf_op jit(solution)/shard_map/convert_element_type | solution.py:67
  157.8 41.7 %while.14 = (s32[]{:T(128)}, bf16[4,512,128]{1,2,0:T(8,128)(2,1)}, bf16[4,512,2048]{2,1,0:T(8,128)(2,1)}, bf16[4,512,2048]{2,1,0:T(8,128)(2,1)}, bf16[4,512,128]...) while((s32[]{:T(128)}, bf16[4,512,128]{1,2,0:T(8,128)(2,1)}, ...), condition=%wide.region_5.6_spmd, body=%wide.region_2.5_spmd.sunk | while | flops 820313088 | bytes 65812748 | solution.py:94
  161.0 5.0 %fusion.134 = bf16[4,512,2048]{2,1,0:T(8,128)(2,1)} fusion(bf16[4,512,2048]{2,1,0:T(8,128)(2,1)} %get-tuple-element.237, s32[]{:T(128)} %get-tuple-element.234, bf16[2048,128]{1,0:T(8,128)(2,1)} %get-tuple-element.249, f32[512]{0:T(512)S(1)} %multiply_reduce_fusion.7, bf16[4,512,128]{2,1,0:T(8,128)(2,1)S(1)} %copy-done.2, ...), kind=kOutput, calls=%fused_computation.5.clone.1 | convolution fusion | flops 274726912 | bytes 6951936 | tf_op jit(solution)/shard_map/while/body/eval_jaxpr/dot_general | solution.py:88
  171.2 5.1 %fusion.134 = bf16[4,512,2048]{2,1,0:T(8,128)(2,1)} fusion(bf16[4,512,2048]{2,1,0:T(8,128)(2,1)} %get-tuple-element.237, s32[]{:T(128)} %get-tuple-element.234, bf16[2048,128]{1,0:T(8,128)(2,1)} %get-tuple-element.249, f32[512]{0:T(512)S(1)} %multiply_reduce_fusion.7, bf16[4,512,128]{2,1,0:T(8,128)(2,1)S(1)} %copy-done.2, ...), kind=kOutput, calls=%fused_computation.5.clone.1 | convolution fusion | flops 274726912 | bytes 6951936 | tf_op jit(solution)/shard_map/while/body/eval_jaxpr/dot_general | solution.py:88
  181.6 5.0 %fusion.134 = bf16[4,512,2048]{2,1,0:T(8,128)(2,1)} fusion(bf16[4,512,2048]{2,1,0:T(8,128)(2,1)} %get-tuple-element.237, s32[]{:T(128)} %get-tuple-element.234, bf16[2048,128]{1,0:T(8,128)(2,1)} %get-tuple-element.249, f32[512]{0:T(512)S(1)} %multiply_reduce_fusion.7, bf16[4,512,128]{2,1,0:T(8,128)(2,1)S(1)} %copy-done.2, ...), kind=kOutput, calls=%fused_computation.5.clone.1 | convolution fusion | flops 274726912 | bytes 6951936 | tf_op jit(solution)/shard_map/while/body/eval_jaxpr/dot_general | solution.py:88
  191.9 5.0 %fusion.134 = bf16[4,512,2048]{2,1,0:T(8,128)(2,1)} fusion(bf16[4,512,2048]{2,1,0:T(8,128)(2,1)} %get-tuple-element.237, s32[]{:T(128)} %get-tuple-element.234, bf16[2048,128]{1,0:T(8,128)(2,1)} %get-tuple-element.249, f32[512]{0:T(512)S(1)} %multiply_reduce_fusion.7, bf16[4,512,128]{2,1,0:T(8,128)(2,1)S(1)} %copy-done.2, ...), kind=kOutput, calls=%fused_computation.5.clone.1 | convolution fusion | flops 274726912 | bytes 6951936 | tf_op jit(solution)/shard_map/while/body/eval_jaxpr/dot_general | solution.py:88
  199.7 10.5 %fusion.57 = f32[2048,128]{0,1:T(8,128)S(1)} fusion(bf16[2048,2048]{1,0:T(8,128)(2,1)} %bitcast.232, bf16[2048,1,128]{0,2,1:T(8,128)(2,1)S(1)} %get-tuple-element.114, f32[2048,1,1]{0,2,1:T(1,128)} %get-tuple-element.140, f32[2048,1,127]{0,2,1:T(8,128)} %get-tuple-element.146, f32[2048,1,127]{0,2,1:T(8,128)S(1)} %copy-done.12, ...), kind=kOutput, calls=%fused_computation.97 | convolution fusion | flops 1077936128 | bytes 12087168 | tf_op jit(solution)/shard_map/dot_general | solution.py:99
  210.3 9.0 %fusion.47 = (f32[2048,128]{0,1:T(8,128)S(1)}, f32[2048,128]{0,1:T(8,128)S(1)}, f32[2048,128]{0,1:T(8,128)S(1)}) fusion(f32[2048]{0:T(1024)S(1)} %copy-done.26, f32[128]{0:T(128)S(1)} %copy-done.50, f32[2048]{0:T(1024)S(1)} %copy-done.24, pred[128]{0:T(512)(128)(4,1)S(1)} %copy-done.53, pred[128]{0:T(512)(128)(4,1)S(1)} %copy-done.47, ...), kind=kOutput, calls=%fused_computation.85 | convolution fusion | flops 1079508992 | bytes 15232896 | tf_op jit(solution)/shard_map/dot_general | solution.py:100
  220.0 9.2 %multiply_reduce_fusion.3 = (f32[128]{0:T(128)S(1)}, f32[128]{0:T(128)S(1)}, f32[2048]{0:T(1024)S(1)}, f32[2048]{0:T(1024)S(1)}, f32[128]{0:T(128)S(1)}, /*index...) fusion(bf16[2048,1,128]{0,2,1:T(8,128)(2,1)S(1)} %get-tuple-element.114, f32[2048]{0:T(1024)S(1)} %copy-done.29, ...), kind=kLoop, calls=%fused_computation.75 | loop fusion | flops 9956864 | bytes 9509760 | tf_op jit(solution)/shard_map/reduce_sum | solution.py:107
  235.5 12.1 %all-to-all-start.5 = ((bf16[1,256,4,128]{3,2,0,1:T(4,128)(2,1)}), bf16[1,256,4,128]{3,2,0,1:T(4,128)(2,1)S(1)}, u32[]{:S(2)}, u32[]{:S(2)}) async-start(bf16[1,256,4,128]{3,2,0,1:T(4,128)(2,1)} %copy.84), calls=%async_computation.5 | async-start | bytes 524288 | tf_op jit(solution)/shard_map/all_to_all | solution.py:150
  249.1 4.1 %copy.81 = bf16[1,1792,4,128]{3,2,0,1:T(4,128)(2,1)} copy(bf16[1,1792,4,128]{1,3,2,0:T(8,128)(2,1)} %slice_bitcast_fusion) | data formatting | bytes 3670016 | tf_op jit(solution)/shard_map/broadcast_in_dim | solution.py:147
  256.2 5.0 %all-to-all-start.4 = ((bf16[1,1792,4,128]{3,2,0,1:T(4,128)(2,1)}), bf16[1,1792,4,128]{3,2,0,1:T(4,128)(2,1)S(1)}, u32[]{:S(2)}, u32[]{:S(2)}) async-start(bf16[1,1792,4,128]{3,2,0,1:T(4,128)(2,1)} %copy.81), calls=%async_computation.4 | async-start | bytes 3670016 | tf_op jit(solution)/shard_map/all_to_all | solution.py:149
  263.1 92.2 %all-reduce = f32[512]{0:T(512)S(1)} all-reduce(f32[512]{0:T(512)S(1)} %fusion.101), channel_id=2, replica_groups=mesh['dp'=32,'seq'=16] {'dp'}, use_global_device_ids=true, to_apply=%region_13.14.clone | all-reduce | flops 512 | bytes 4096
  355.4 39.0 %psum.8 = f32[16]{0:T(128)} all-reduce(f32[16]{0:T(128)S(1)} %dynamic-slice.1), channel_id=1, replica_groups=mesh['dp'=32,'seq'=16] {'seq'}, use_global_device_ids=true, to_apply=%region_12.13 | all-reduce | flops 16 | bytes 128 | tf_op jit(solution)/shard_map/psum | solution.py:158
  (262 shorter events, 92.6 us)
Async XLA Ops:
  15.9 17.3 %all-to-all-start.2 = ((bf16[16,2,1024]{2,1,0:T(2,128)(2,1)}), bf16[16,2,1024]{2,1,0:T(2,128)(2,1)S(1)}, u32[]{:S(2)}, u32[]{:S(2)}) async-start(bf16[16,2,1024]{2,1,0:T(2,128)(2,1)} %reshape.852), calls=%async_computation.2 | async-start | bytes 131072 | tf_op jit(solution)/shard_map/all_to_all | solution.py:127
  28.7 33.9 %copy-start.11 = (bf16[1,112,3,2048]{3,1,2,0:T(8,128)(2,1)S(1)}, bf16[1,112,3,2048]{3,1,2,0:T(8,128)(2,1)}, u32[]{:S(2)}) copy-start(bf16[1,112,3,2048]{3,1,2,0:T(8,128)(2,1)} %param.7) | copy-start | bytes 4128772
  33.2 21.8 %all-to-all-start = ((bf16[16,2,3072]{2,1,0:T(2,128)(2,1)}), bf16[16,2,3072]{2,1,0:T(2,128)(2,1)S(1)}, u32[]{:S(2)}, u32[]{:S(2)}) async-start(bf16[16,2,3072]{2,1,0:T(2,128)(2,1)} %reshape.848), calls=%async_computation | async-start | bytes 393216 | tf_op jit(solution)/shard_map/all_to_all | solution.py:123
  55.0 28.7 %copy-start.57 = (f32[4,128]{1,0:T(4,128)S(1)}, f32[4,128]{1,0:T(4,128)}, u32[]{:S(2)}) copy-start(f32[4,128]{1,0:T(4,128)} %param.11) | copy-start | bytes 6148
  55.0 19.4 %copy-start.15 = (bf16[16,2,3072]{2,1,0:T(2,128)(2,1)}, bf16[16,2,3072]{2,1,0:T(2,128)(2,1)S(1)}, u32[]{:S(2)}) copy-start(bf16[16,2,3072]{2,1,0:T(2,128)(2,1)S(1)} %all-to-all-done) | copy-start | bytes 589828
  55.0 19.4 %all-to-all-start.3 = ((bf16[16,2,7168]{2,1,0:T(2,128)(2,1)}), bf16[16,2,7168]{2,1,0:T(2,128)(2,1)S(1)}, u32[]{:S(2)}, u32[]{:S(2)}) async-start(bf16[16,2,7168]{2,1,0:T(2,128)(2,1)} %reshape.850), calls=%async_computation.3 | async-start | bytes 917504 | tf_op jit(solution)/shard_map/all_to_all | solution.py:126
  75.1 45.9 %all-to-all-start.1 = ((bf16[1,112,3,2048]{1,2,0,3:T(4,128)(2,1)}), bf16[1,112,3,2048]{1,2,0,3:T(4,128)(2,1)S(1)}, u32[]{:S(2)}, u32[]{:S(2)}) async-start(bf16[1,112,3,2048]{1,2,0,3:T(4,128)(2,1)} %copy.60), calls=%async_computation.1 | async-start | bytes 4194304 | tf_op jit(solution)/shard_map/all_to_all | solution.py:122
  81.2 46.7 %copy-start.45 = (pred[128]{0:T(512)(128)(4,1)}, pred[128]{0:T(512)(128)(4,1)S(1)}, u32[]{:S(2)}) copy-start(pred[128]{0:T(512)(128)(4,1)S(1)} %iota_compare_fusion.1) | copy-start | bytes 388
  81.2 46.7 %copy-start.48 = (f32[128]{0:T(128)}, f32[128]{0:T(128)S(1)}, u32[]{:S(2)}) copy-start(f32[128]{0:T(128)S(1)} %multiply_power_fusion) | copy-start | bytes 1540
  81.2 46.6 %copy-start.51 = (pred[128]{0:T(512)(128)(4,1)}, pred[128]{0:T(512)(128)(4,1)S(1)}, u32[]{:S(2)}) copy-start(pred[128]{0:T(512)(128)(4,1)S(1)} %get-tuple-element.162) | copy-start | bytes 388
  81.3 46.6 %copy-start.54 = (pred[128]{0:T(512)(128)(4,1)}, pred[128]{0:T(512)(128)(4,1)S(1)}, u32[]{:S(2)}) copy-start(pred[128]{0:T(512)(128)(4,1)S(1)} %get-tuple-element.163) | copy-start | bytes 388
  83.0 44.9 %copy-start.23 = (f32[2048]{0:T(1024)}, f32[2048]{0:T(1024)S(1)}, u32[]{:S(2)}) copy-start(f32[2048]{0:T(1024)S(1)} %get-tuple-element.160) | copy-start | bytes 24580
  83.0 44.9 %copy-start.25 = (f32[2048]{0:T(1024)}, f32[2048]{0:T(1024)S(1)}, u32[]{:S(2)}) copy-start(f32[2048]{0:T(1024)S(1)} %get-tuple-element.161) | copy-start | bytes 24580
  83.7 44.2 %copy-start.31 = (f32[128]{0:T(128)}, f32[128]{0:T(128)S(1)}, u32[]{:S(2)}) copy-start(f32[128]{0:T(128)S(1)} %get-tuple-element.153) | copy-start | bytes 1540
  83.7 44.2 %copy-start.33 = (f32[128]{0:T(128)}, f32[128]{0:T(128)S(1)}, u32[]{:S(2)}) copy-start(f32[128]{0:T(128)S(1)} %get-tuple-element.154) | copy-start | bytes 1540
  83.7 44.2 %copy-start.36 = (f32[128]{0:T(128)}, f32[128]{0:T(128)S(1)}, u32[]{:S(2)}) copy-start(f32[128]{0:T(128)S(1)} %get-tuple-element.155) | copy-start | bytes 1540
  83.7 44.2 %copy-start.40 = (f32[128]{0:T(128)}, f32[128]{0:T(128)S(1)}, u32[]{:S(2)}) copy-start(f32[128]{0:T(128)S(1)} %get-tuple-element.156) | copy-start | bytes 1540
  85.2 12.4 %copy-start.18 = (bf16[1,16,16,128]{3,2,1,0:T(8,128)(2,1)}, bf16[1,16,16,128]{3,2,1,0:T(8,128)(2,1)S(1)}, u32[]{:S(2)}) copy-start(bf16[1,16,16,128]{3,2,1,0:T(8,128)(2,1)S(1)} %copy.72) | copy-start | bytes 196612
  92.3 32.8 %copy-start.10 = (bf16[256,3,128]{0,2,1:T(8,128)(2,1)}, bf16[256,3,128]{0,2,1:T(8,128)(2,1)S(1)}, u32[]{:S(2)}) copy-start(bf16[256,3,128]{0,2,1:T(8,128)(2,1)S(1)} %copy.63) | copy-start | bytes 589828
  138.7 11.3 %copy-start.37 = (f32[128]{0:T(128)S(1)}, f32[128]{0:T(128)}, u32[]{:S(2)}) copy-start(f32[128]{0:T(128)} %copy-done.36) | copy-start | bytes 1540
  138.7 11.3 %copy-start.42 = (pred[4,512]{1,0:T(4,128)(4,1)S(1)}, pred[4,512]{1,0:T(4,128)(4,1)}, u32[]{:S(2)}) copy-start(pred[4,512]{1,0:T(4,128)(4,1)} %convert_compare_fusion) | copy-start | bytes 6148
  157.8 41.7 %copy-start.12 = (f32[2048,1,127]{0,2,1:T(8,128)S(1)}, f32[2048,1,127]{0,2,1:T(8,128)}, u32[]{:S(2)}) copy-start(f32[2048,1,127]{0,2,1:T(8,128)} %get-tuple-element.143) | copy-start | bytes 3121156
  235.5 20.7 %all-to-all-start.5 = ((bf16[1,256,4,128]{3,2,0,1:T(4,128)(2,1)}), bf16[1,256,4,128]{3,2,0,1:T(4,128)(2,1)S(1)}, u32[]{:S(2)}, u32[]{:S(2)}) async-start(bf16[1,256,4,128]{3,2,0,1:T(4,128)(2,1)} %copy.84), calls=%async_computation.5 | async-start | bytes 524288 | tf_op jit(solution)/shard_map/all_to_all | solution.py:150
  256.2 139.6 %all-to-all-start.4 = ((bf16[1,1792,4,128]{3,2,0,1:T(4,128)(2,1)}), bf16[1,1792,4,128]{3,2,0,1:T(4,128)(2,1)S(1)}, u32[]{:S(2)}, u32[]{:S(2)}) async-start(bf16[1,1792,4,128]{3,2,0,1:T(4,128)(2,1)} %copy.81), calls=%async_computation.4 | async-start | bytes 3670016 | tf_op jit(solution)/shard_map/all_to_all | solution.py:149
  (61 other events, 352.0 us)
where the time goes:
time: 406 us; the launch traced here: 399 us
  blocking collectives  131 us (32%)
  local copies, waits for them, and re-layouts  67.2 us (17%)
  other arithmetic  62.7 us (15%)
  matrix products  51.8 us (13%)
  starting transfers between devices  47.1 us (12%)
  waiting for transfers between devices  35.8 us (9%)
    unnamed x1, blocking collectives  92.2 us
    psum x1, blocking collectives, per_device(): summed = lax.psum(partial_grad, 'seq')  39 us
    unnamed x125, local copies, waits for them, and re-layouts  27.8 us
    unnamed x3, other arithmetic  23.1 us
    all_to_all x1, waiting for transfers between devices, per_device(): lax.all_to_all(img_qkv, 'seq', split_axis=3, concat_axis=1, tiled=True)  21.8 us
    dot_general x4, matrix products, block_step(): lax.dot_general(d_block, value, contract_last, preferred_element_type=jnp...  20.2 us
    all_to_all x1, starting transfers between devices, per_device(): lax.all_to_all(txt_back, 'seq', split_axis=1, concat_axis=3, tiled=True)  12.1 us
    dot_general x1, matrix products, head_pass(): dq_rot = jnp.dot(d_score_all, k_rot, preferred_element_type=jnp.float32)  10.5 us
  transfers between devices with their start and end apart: 6, of which 4 were waited for; matrix products, arithmetic and copies ran while one was open for 12% of the time, Pallas kernels for 0%

commit v1 on v0

--- a/solution.py
+++ b/solution.py
@@ -155,7 +155,7 @@
     txt_grad = txt_tokens[:, :, 0:3, :]
     grad_scale = 1.0 / math.sqrt(data_devices * seq_len * local_heads * seq_devices)
     partial_grad = (gain_terms * grad_scale).reshape(4 * head_dim)
-    summed = lax.psum(partial_grad, "seq")
+    summed = jnp.sum(lax.all_gather(partial_grad, "seq"), 0)
     gain_grad = lax.psum_scatter(summed, "dp", scatter_dimension=0, tiled=True)
     return (img_out, txt_out, img_grad, txt_grad, gain_grad)
 

time: 406 us -> 424 us (1.044)
  the two profiles are of different devices: /device:TPU:2 before, /device:TPU:128 now
where the time goes in v1:
time: 424 us; the launch traced here: 417 us
  blocking collectives  150 us (35%)
  local copies, waits for them, and re-layouts  66.6 us (16%)
  other arithmetic  62.9 us (15%)
  matrix products  51.9 us (12%)
  waiting for transfers between devices  42.6 us (10%)
  starting transfers between devices  39.9 us (9%)
    unnamed x1, blocking collectives  86 us
    all_gather x1, blocking collectives, per_device(): summed = jnp.sum(lax.all_gather(partial_grad, 'seq'), 0)  64.4 us
    all_to_all x1, waiting for transfers between devices, per_device(): lax.all_to_all(img_qkv, 'seq', split_axis=3, concat_axis=1, tiled=True)  31.6 us
    unnamed x107, local copies, waits for them, and re-layouts  27.2 us
    unnamed x3, other arithmetic  23.1 us
    dot_general x4, matrix products, block_step(): lax.dot_general(d_block, value, contract_last, preferred_element_type=jnp...  20.2 us
    dot_general x1, matrix products, head_pass(): dq_rot = jnp.dot(d_score_all, k_rot, preferred_element_type=jnp.float32)  10.5 us
    concatenate x6, local copies, waits for them, and re-layouts, rotate(): preceding = jnp.roll(values_in, 1, axis=-1)  9.45 us
  transfers between devices with their start and end apart: 6, of which 4 were waited for; matrix products, arithmetic and copies ran while one was open for 12% of the time, Pallas kernels for 0%

profile of v1, /device:TPU:128, one launch (start us, length us, event | category | flops | bytes accessed | tf_op | source)
XLA Modules:
  0.0 417.4 jit_solution(6558847438648021533)
XLA Ops:
  3.1 11.5 %reduce.10 = bf16[2048,16]{1,0:T(8,128)(2,1)S(1)} reduce(bf16[2048,1,16]{2,1,0:T(2,128)(2,1)S(1)} %bitcast.204, bf16[]{:T(256)} %broadcast.818), dimensions={1}, to_apply=%bitcast.164.reduce_sub_computation | reduce | bytes 131074
  15.9 8.5 %all-to-all-start.2 = ((bf16[16,2,1024]{2,1,0:T(2,128)(2,1)}), bf16[16,2,1024]{2,1,0:T(2,128)(2,1)S(1)}, u32[]{:S(2)}, u32[]{:S(2)}) async-start(bf16[16,2,1024]{2,1,0:T(2,128)(2,1)} %reshape.863), calls=%async_computation.2 | async-start | bytes 131072 | tf_op jit(solution)/shard_map/all_to_all | solution.py:127
  30.1 7.3 %all-to-all-start = ((bf16[16,2,3072]{2,1,0:T(2,128)(2,1)}), bf16[16,2,3072]{2,1,0:T(2,128)(2,1)S(1)}, u32[]{:S(2)}, u32[]{:S(2)}) async-start(bf16[16,2,3072]{2,1,0:T(2,128)(2,1)} %reshape.859), calls=%async_computation | async-start | bytes 393216 | tf_op jit(solution)/shard_map/all_to_all | solution.py:123
  39.8 11.5 %reduce.9 = bf16[2048,112]{1,0:T(8,128)(2,1)S(1)} reduce(bf16[2048,1,112]{2,1,0:T(2,128)(2,1)S(1)} %bitcast.205, bf16[]{:T(256)} %broadcast.818), dimensions={1}, to_apply=%bitcast.162.reduce_sub_computation | reduce | bytes 917506
  53.2 7.7 %all-to-all-start.3 = ((bf16[16,2,7168]{2,1,0:T(2,128)(2,1)}), bf16[16,2,7168]{2,1,0:T(2,128)(2,1)S(1)}, u32[]{:S(2)}, u32[]{:S(2)}) async-start(bf16[16,2,7168]{2,1,0:T(2,128)(2,1)} %reshape.861), calls=%async_computation.3 | async-start | bytes 917504 | tf_op jit(solution)/shard_map/all_to_all | solution.py:126
  60.8 4.1 copy.60
  64.9 7.9 %all-to-all-done.3 = bf16[16,2,7168]{2,1,0:T(2,128)(2,1)S(1)} async-done(((bf16[16,2,7168]{2,1,0:T(2,128)(2,1)}), bf16[16,2,7168]{2,1,0:T(2,128)(2,1)S(1)}, u32[]{:S(2)}, u32[]{:S(2)}) %all-to-all-start.3) | async-done | bytes 458784 | tf_op jit(solution)/shard_map/all_to_all | solution.py:126
  72.9 5.7 %all-to-all-start.1 = ((bf16[1,112,3,2048]{1,2,0,3:T(4,128)(2,1)}), bf16[1,112,3,2048]{1,2,0,3:T(4,128)(2,1)S(1)}, u32[]{:S(2)}, u32[]{:S(2)}) async-start(bf16[1,112,3,2048]{1,2,0,3:T(4,128)(2,1)} %copy.60), calls=%async_computation.1 | async-start | bytes 4194304 | tf_op jit(solution)/shard_map/all_to_all | solution.py:122
  93.8 31.6 %all-to-all-done.1 = bf16[1,112,3,2048]{1,2,0,3:T(4,128)(2,1)S(1)} async-done(((bf16[1,112,3,2048]{1,2,0,3:T(4,128)(2,1)}), bf16[1,112,3,2048]{1,2,0,3:T(4,128)(2,1)S(1)}, u32[]{:S(2)}, u32[]{:S(2)}) %all-to-all-start.1) | async-done | bytes 1376288 | tf_op jit(solution)/shard_map/all_to_all | solution.py:122
  132.3 6.0 %fusion.33 = (bf16[2048,128]{0,1:T(8,128)(2,1)}, f32[2048,128]{0,1:T(8,128)S(1)}) fusion(f32[2048,1]{0,1:T(1,128)S(1)} %get-tuple-element.142, f32[2048,127]{0,1:T(8,128)S(1)} %get-tuple-element.145, f32[2048,127]{0,1:T(8,128)S(1)} %get-tuple-element.144, f32[2048,1]{0,1:T(1,128)S(1)} %get-tuple-element.141, f32[2048]{0:T(1024)S(1)} %get-tuple-element.161, ...), kind=kLoop, calls=%fused_computation.55 | loop fusion | flops 5242880 | bytes 4756352 | tf_op jit(solution)/shard_map/convert_element_type | solution.py:68
  154.3 7.8 %fusion.29 = bf16[4,512,128]{2,1,0:T(8,128)(2,1)S(1)} fusion(f32[4,512,1]{2,1,0:T(8,128)} %concatenate.120, f32[4,512,127]{2,1,0:T(8,128)} %bitcast.209, f32[4,512,127]{2,1,0:T(8,128)} %bitcast.210, f32[4,512,1]{2,1,0:T(8,128)} %concatenate.121, f32[4,512,128]{2,1,0:T(8,128)S(1)} %bitcast.208, f32[4,512]{1,0:T(4,128)S(1)} %get-tuple-element.165, ...), kind=kLoop, calls=%fused_computation.50 | loop fusion | flops 3932160 | bytes 3698560 | tf_op jit(solution)/shard_map/convert_element_type | solution.py:67
  162.1 41.9 %while.14 = (s32[]{:T(128)}, bf16[4,512,128]{1,2,0:T(8,128)(2,1)}, bf16[4,512,2048]{2,1,0:T(8,128)(2,1)}, bf16[4,512,2048]{2,1,0:T(8,128)(2,1)}, bf16[4,512,128]...) while((s32[]{:T(128)}, bf16[4,512,128]{1,2,0:T(8,128)(2,1)}, ...), condition=%wide.region_5.6_spmd, body=%wide.region_2.5_spmd.sunk | while | flops 820313088 | bytes 65812748 | solution.py:94
  165.3 5.1 %fusion.133 = bf16[4,512,2048]{2,1,0:T(8,128)(2,1)} fusion(bf16[4,512,2048]{2,1,0:T(8,128)(2,1)} %get-tuple-element.237, s32[]{:T(128)} %get-tuple-element.234, bf16[2048,128]{1,0:T(8,128)(2,1)} %get-tuple-element.249, f32[512]{0:T(512)S(1)} %multiply_reduce_fusion.7, bf16[4,512,128]{2,1,0:T(8,128)(2,1)S(1)} %copy-done.3, ...), kind=kOutput, calls=%fused_computation.5.clone.1 | convolution fusion | flops 274726912 | bytes 6951936 | tf_op jit(solution)/shard_map/while/body/eval_jaxpr/dot_general | solution.py:88
  175.6 5.1 %fusion.133 = bf16[4,512,2048]{2,1,0:T(8,128)(2,1)} fusion(bf16[4,512,2048]{2,1,0:T(8,128)(2,1)} %get-tuple-element.237, s32[]{:T(128)} %get-tuple-element.234, bf16[2048,128]{1,0:T(8,128)(2,1)} %get-tuple-element.249, f32[512]{0:T(512)S(1)} %multiply_reduce_fusion.7, bf16[4,512,128]{2,1,0:T(8,128)(2,1)S(1)} %copy-done.3, ...), kind=kOutput, calls=%fused_computation.5.clone.1 | convolution fusion | flops 274726912 | bytes 6951936 | tf_op jit(solution)/shard_map/while/body/eval_jaxpr/dot_general | solution.py:88
  186.0 5.0 %fusion.133 = bf16[4,512,2048]{2,1,0:T(8,128)(2,1)} fusion(bf16[4,512,2048]{2,1,0:T(8,128)(2,1)} %get-tuple-element.237, s32[]{:T(128)} %get-tuple-element.234, bf16[2048,128]{1,0:T(8,128)(2,1)} %get-tuple-element.249, f32[512]{0:T(512)S(1)} %multiply_reduce_fusion.7, bf16[4,512,128]{2,1,0:T(8,128)(2,1)S(1)} %copy-done.3, ...), kind=kOutput, calls=%fused_computation.5.clone.1 | convolution fusion | flops 274726912 | bytes 6951936 | tf_op jit(solution)/shard_map/while/body/eval_jaxpr/dot_general | solution.py:88
  196.3 5.0 %fusion.133 = bf16[4,512,2048]{2,1,0:T(8,128)(2,1)} fusion(bf16[4,512,2048]{2,1,0:T(8,128)(2,1)} %get-tuple-element.237, s32[]{:T(128)} %get-tuple-element.234, bf16[2048,128]{1,0:T(8,128)(2,1)} %get-tuple-element.249, f32[512]{0:T(512)S(1)} %multiply_reduce_fusion.7, bf16[4,512,128]{2,1,0:T(8,128)(2,1)S(1)} %copy-done.3, ...), kind=kOutput, calls=%fused_computation.5.clone.1 | convolution fusion | flops 274726912 | bytes 6951936 | tf_op jit(solution)/shard_map/while/body/eval_jaxpr/dot_general | solution.py:88
  204.1 10.5 %fusion.57 = f32[2048,128]{0,1:T(8,128)S(1)} fusion(bf16[2048,2048]{1,0:T(8,128)(2,1)} %bitcast.232, bf16[2048,1,128]{0,2,1:T(8,128)(2,1)S(1)} %get-tuple-element.114, f32[2048,1,1]{0,2,1:T(1,128)} %get-tuple-element.140, f32[2048,1,127]{0,2,1:T(8,128)} %get-tuple-element.146, f32[2048,1,127]{0,2,1:T(8,128)S(1)} %copy-done.12, ...), kind=kOutput, calls=%fused_computation.97 | convolution fusion | flops 1077936128 | bytes 12087168 | tf_op jit(solution)/shard_map/dot_general | solution.py:99
  214.7 9.1 %fusion.47 = (f32[2048,128]{0,1:T(8,128)S(1)}, f32[2048,128]{0,1:T(8,128)S(1)}, f32[2048,128]{0,1:T(8,128)S(1)}) fusion(f32[2048]{0:T(1024)S(1)} %copy-done.25, f32[128]{0:T(128)S(1)} %copy-done.42, f32[2048]{0:T(1024)S(1)} %copy-done.23, pred[128]{0:T(512)(128)(4,1)S(1)} %copy-done.44, pred[128]{0:T(512)(128)(4,1)S(1)} %copy-done.40, ...), kind=kOutput, calls=%fused_computation.85 | convolution fusion | flops 1079508992 | bytes 15232896 | tf_op jit(solution)/shard_map/dot_general | solution.py:100
  224.6 9.2 %multiply_reduce_fusion.3 = (f32[128]{0:T(128)S(1)}, f32[128]{0:T(128)S(1)}, f32[2048]{0:T(1024)S(1)}, f32[2048]{0:T(1024)S(1)}, f32[128]{0:T(128)S(1)}, /*index...) fusion(bf16[2048,1,128]{0,2,1:T(8,128)(2,1)S(1)} %get-tuple-element.114, f32[2048]{0:T(1024)S(1)} %copy-done.26, ...), kind=kLoop, calls=%fused_computation.75 | loop fusion | flops 9956864 | bytes 9509760 | tf_op jit(solution)/shard_map/reduce_sum | solution.py:107
  241.3 5.2 %all-to-all-start.5 = ((bf16[1,256,4,128]{3,2,0,1:T(4,128)(2,1)}), bf16[1,256,4,128]{3,2,0,1:T(4,128)(2,1)S(1)}, u32[]{:S(2)}, u32[]{:S(2)}) async-start(bf16[1,256,4,128]{3,2,0,1:T(4,128)(2,1)} %copy.84), calls=%async_computation.5 | async-start | bytes 524288 | tf_op jit(solution)/shard_map/all_to_all | solution.py:150
  247.8 4.1 copy.81
  254.5 5.6 %all-to-all-start.4 = ((bf16[1,1792,4,128]{3,2,0,1:T(4,128)(2,1)}), bf16[1,1792,4,128]{3,2,0,1:T(4,128)(2,1)S(1)}, u32[]{:S(2)}, u32[]{:S(2)}) async-start(bf16[1,1792,4,128]{3,2,0,1:T(4,128)(2,1)} %copy.81), calls=%async_computation.4 | async-start | bytes 3670016 | tf_op jit(solution)/shard_map/all_to_all | solution.py:149
  262.0 64.4 %all-gather = f32[16,1,512]{2,1,0:T(1,128)S(1)} all-gather(f32[1,1,512]{2,1,0:T(1,128)S(1)} %bitcast.224), channel_id=1, replica_groups=mesh['dp'=32,'seq'=16] {'seq'}, dimensions={0}, use_global_device_ids=true | all-gather | bytes 34816 | tf_op jit(solution)/shard_map/all_gather | solution.py:158
  326.5 86.0 %all-reduce = f32[512]{0:T(512)S(1)} all-reduce(f32[512]{0:T(512)S(1)} %reduce_sum.107), channel_id=2, replica_groups=mesh['dp'=32,'seq'=16] {'dp'}, use_global_device_ids=true, to_apply=%region_13.14.clone | all-reduce | flops 512 | bytes 4096
  (245 shorter events, 90.5 us)
Async XLA Ops:
  15.9 14.3 %all-to-all-start.2 = ((bf16[16,2,1024]{2,1,0:T(2,128)(2,1)}), bf16[16,2,1024]{2,1,0:T(2,128)(2,1)S(1)}, u32[]{:S(2)}, u32[]{:S(2)}) async-start(bf16[16,2,1024]{2,1,0:T(2,128)(2,1)} %reshape.863), calls=%async_computation.2 | async-start | bytes 131072 | tf_op jit(solution)/shard_map/all_to_all | solution.py:127
  30.1 23.0 %all-to-all-start = ((bf16[16,2,3072]{2,1,0:T(2,128)(2,1)}), bf16[16,2,3072]{2,1,0:T(2,128)(2,1)S(1)}, u32[]{:S(2)}, u32[]{:S(2)}) async-start(bf16[16,2,3072]{2,1,0:T(2,128)(2,1)} %reshape.859), calls=%async_computation | async-start | bytes 393216 | tf_op jit(solution)/shard_map/all_to_all | solution.py:123
  53.2 26.8 %copy-start.48 = (f32[4,128]{1,0:T(4,128)S(1)}, f32[4,128]{1,0:T(4,128)}, u32[]{:S(2)}) copy-start(f32[4,128]{1,0:T(4,128)} %param.11) | copy-start | bytes 6148
  53.2 19.7 %all-to-all-start.3 = ((bf16[16,2,7168]{2,1,0:T(2,128)(2,1)}), bf16[16,2,7168]{2,1,0:T(2,128)(2,1)S(1)}, u32[]{:S(2)}, u32[]{:S(2)}) async-start(bf16[16,2,7168]{2,1,0:T(2,128)(2,1)} %reshape.861), calls=%async_computation.3 | async-start | bytes 917504 | tf_op jit(solution)/shard_map/all_to_all | solution.py:126
  72.9 52.6 %all-to-all-start.1 = ((bf16[1,112,3,2048]{1,2,0,3:T(4,128)(2,1)}), bf16[1,112,3,2048]{1,2,0,3:T(4,128)(2,1)S(1)}, u32[]{:S(2)}, u32[]{:S(2)}) async-start(bf16[1,112,3,2048]{1,2,0,3:T(4,128)(2,1)} %copy.60), calls=%async_computation.1 | async-start | bytes 4194304 | tf_op jit(solution)/shard_map/all_to_all | solution.py:122
  78.6 75.6 %copy-start.39 = (pred[128]{0:T(512)(128)(4,1)}, pred[128]{0:T(512)(128)(4,1)S(1)}, u32[]{:S(2)}) copy-start(pred[128]{0:T(512)(128)(4,1)S(1)} %iota_compare_fusion.1) | copy-start | bytes 388
  78.7 75.6 %copy-start.41 = (f32[128]{0:T(128)}, f32[128]{0:T(128)S(1)}, u32[]{:S(2)}) copy-start(f32[128]{0:T(128)S(1)} %multiply_power_fusion) | copy-start | bytes 1540
  78.7 53.6 %copy-start.45 = (pred[128]{0:T(512)(128)(4,1)}, pred[128]{0:T(512)(128)(4,1)S(1)}, u32[]{:S(2)}) copy-start(pred[128]{0:T(512)(128)(4,1)S(1)} %get-tuple-element.163) | copy-start | bytes 388
  78.7 75.6 %copy-start.43 = (pred[128]{0:T(512)(128)(4,1)}, pred[128]{0:T(512)(128)(4,1)S(1)}, u32[]{:S(2)}) copy-start(pred[128]{0:T(512)(128)(4,1)S(1)} %get-tuple-element.162) | copy-start | bytes 388
  79.9 52.4 %copy-start.22 = (f32[2048]{0:T(1024)}, f32[2048]{0:T(1024)S(1)}, u32[]{:S(2)}) copy-start(f32[2048]{0:T(1024)S(1)} %get-tuple-element.160) | copy-start | bytes 24580
  79.9 52.4 %copy-start.24 = (f32[2048]{0:T(1024)}, f32[2048]{0:T(1024)S(1)}, u32[]{:S(2)}) copy-start(f32[2048]{0:T(1024)S(1)} %get-tuple-element.161) | copy-start | bytes 24580
  80.0 52.3 %copy-start.28 = (f32[128]{0:T(128)}, f32[128]{0:T(128)S(1)}, u32[]{:S(2)}) copy-start(f32[128]{0:T(128)S(1)} %get-tuple-element.153) | copy-start | bytes 1540
  80.0 52.3 %copy-start.35 = (f32[128]{0:T(128)}, f32[128]{0:T(128)S(1)}, u32[]{:S(2)}) copy-start(f32[128]{0:T(128)S(1)} %get-tuple-element.156) | copy-start | bytes 1540
  80.0 74.2 %copy-start.30 = (f32[128]{0:T(128)}, f32[128]{0:T(128)S(1)}, u32[]{:S(2)}) copy-start(f32[128]{0:T(128)S(1)} %get-tuple-element.154) | copy-start | bytes 1540
  80.0 74.2 %copy-start.32 = (f32[128]{0:T(128)}, f32[128]{0:T(128)S(1)}, u32[]{:S(2)}) copy-start(f32[128]{0:T(128)S(1)} %get-tuple-element.155) | copy-start | bytes 1540
  81.5 11.3 %copy-start.17 = (bf16[1,16,16,128]{3,2,1,0:T(8,128)(2,1)}, bf16[1,16,16,128]{3,2,1,0:T(8,128)(2,1)S(1)}, u32[]{:S(2)}) copy-start(bf16[1,16,16,128]{3,2,1,0:T(8,128)(2,1)S(1)} %copy.72) | copy-start | bytes 196612
  87.6 42.0 %copy-start.11 = (bf16[256,3,128]{0,2,1:T(8,128)(2,1)}, bf16[256,3,128]{0,2,1:T(8,128)(2,1)S(1)}, u32[]{:S(2)}) copy-start(bf16[256,3,128]{0,2,1:T(8,128)(2,1)S(1)} %copy.63) | copy-start | bytes 589828
  92.8 34.9 %copy-start.8 = (bf16[1,16,112,128]{3,2,1,0:T(8,128)(2,1)}, bf16[1,16,112,128]{3,2,1,0:T(8,128)(2,1)S(1)}, u32[]{:S(2)}) copy-start(bf16[1,16,112,128]{3,2,1,0:T(8,128)(2,1)S(1)} %copy.75) | copy-start | bytes 1376260
  129.8 11.2 %copy-start.19 = (f32[2048]{0:T(1024)}, f32[2048]{0:T(1024)S(1)}, u32[]{:S(2)}) copy-start(f32[2048]{0:T(1024)S(1)} %get-tuple-element.159) | copy-start | bytes 24580
  143.0 11.3 %copy-start.46 = (pred[128]{0:T(512)(128)(4,1)S(1)}, pred[128]{0:T(512)(128)(4,1)}, u32[]{:S(2)}) copy-start(pred[128]{0:T(512)(128)(4,1)} %copy-done.45) | copy-start | bytes 388
  162.1 41.9 %copy-start.12 = (f32[2048,1,127]{0,2,1:T(8,128)S(1)}, f32[2048,1,127]{0,2,1:T(8,128)}, u32[]{:S(2)}) copy-start(f32[2048,1,127]{0,2,1:T(8,128)} %get-tuple-element.143) | copy-start | bytes 3121156
  204.0 10.6 %copy-start.13 = (f32[2048,1,127]{0,2,1:T(8,128)S(1)}, f32[2048,1,127]{0,2,1:T(8,128)}, u32[]{:S(2)}) copy-start(f32[2048,1,127]{0,2,1:T(8,128)} %get-tuple-element.131) | copy-start | bytes 3121156
  241.3 13.2 %all-to-all-start.5 = ((bf16[1,256,4,128]{3,2,0,1:T(4,128)(2,1)}), bf16[1,256,4,128]{3,2,0,1:T(4,128)(2,1)S(1)}, u32[]{:S(2)}, u32[]{:S(2)}) async-start(bf16[1,256,4,128]{3,2,0,1:T(4,128)(2,1)} %copy.84), calls=%async_computation.5 | async-start | bytes 524288 | tf_op jit(solution)/shard_map/all_to_all | solution.py:150
  254.5 160.0 %all-to-all-start.4 = ((bf16[1,1792,4,128]{3,2,0,1:T(4,128)(2,1)}), bf16[1,1792,4,128]{3,2,0,1:T(4,128)(2,1)S(1)}, u32[]{:S(2)}, u32[]{:S(2)}) async-start(bf16[1,1792,4,128]{3,2,0,1:T(4,128)(2,1)} %copy.81), calls=%async_computation.4 | async-start | bytes 3670016 | tf_op jit(solution)/shard_map/all_to_all | solution.py:149
  (52 other events, 259.3 us)
